TPU v7x, 128 devices: a whole 4x4x4 slice. The times are simulated.
128 devices in a mesh: src: 32 (over x, z, core), tgt: 4 (over y).
Axes of the slice: x: 4, y: 4, z: 4, core: 2. Of those that a mesh axis runs over, the one named last changes fastest.
Arguments:
- src_pts: float32 [3, 512, 256], P(None, 'src'), may hold values from -8 to 9
- src_mass: float32 [512, 256], P('src'), may hold values from 0.25 to 4
- tgt_pts: float32 [3, 256, 1024], P(None, None, 'tgt'), may hold values from -6 to 6
- tgt_mass: float32 [256, 1024], P(None, 'tgt'), may hold values from 0.25 to 4
- listed: int32 [512, 4, 8], P('src', 'tgt'), may hold values from 0 to 255, all different within a row
- live: int32 [512, 4], P('src', 'tgt'), may hold values from 1 to 8, 16 in all within a row
Outputs:
- fine_f: float32 [512, 256], P('src')
- fine_g: float32 [256, 1024], P('src', 'tgt')
Inputs may be any that keep to these rules, and one draw needn't show every extreme that they name: Within one row listed[c, t, :] the entries are distinct; only the first live[c, t] of them are used. For each source cluster c the counts live[c, :] add up to 16.
All inputs are finite; a program needn't handle non-finite values. No bound on the sum of `live` on one device may be relied on, other than what follows from the above.
Results may differ from a plain program's by a relative error of at most 0.0003.
Values sent between devices are 32-bit elements; how exact they have to be, the bound alone decides.
No kernel may reach another device: no remote copies, remote signals or barrier semaphores. Data moves between devices by JAX's collectives and lax.ppermute only.
A program may use at most 128 MiB of HBM per device.

v0:
```python
import jax
import jax.numpy as jnp
from jax import lax
from jax.sharding import PartitionSpec as P

EPS = 0.1
NEG = -1e30


def rows_first(arrays, axis, dims):
    turned = [jnp.moveaxis(a, dim, 0) for a, dim in zip(arrays, dims)]
    widths = [t[0].size for t in turned]
    both = jnp.concatenate([t.reshape(-1, w) for t, w in zip(turned, widths)], axis=1)
    whole = lax.all_gather(both, axis, axis=0, tiled=True)
    tiles = jnp.split(whole, [sum(widths[:k]) for k in range(1, len(widths))], axis=1)
    return tuple(
        (
            jnp.moveaxis(b.reshape(-1, *t.shape[1:]), 0, dim)
            for b, t, dim in zip(tiles, turned, dims)
        )
    )


def collected_together(array, axis):
    leaves = jax.tree.leaves(array)
    order = sorted(range(len(leaves)), key=lambda k: -leaves[k].size)
    width = (1, *leaves[order[0]].shape)[-1]
    lines = [
        jnp.pad(leaves[k].reshape(-1), (0, -leaves[k].size % width)).reshape(-1, width)
        for k in order
    ]
    both, at, found = (lax.all_gather(jnp.concatenate(lines), axis), 0, {})
    for k, line in zip(order, lines):
        share = both[:, at : at + len(line)].reshape(len(both), -1)
        found[k] = share[:, : leaves[k].size].reshape(-1, *leaves[k].shape)
        at += len(line)
    numbers = iter(range(len(leaves)))
    return jax.tree.map(lambda _: found[next(numbers)], array)


def merged(value, axis, join):
    pieces = collected_together(value, axis)
    head = jax.tree.map(lambda part: part[0], pieces)
    tail = jax.tree.map(lambda part: part[1:], pieces)
    subtotal, _ = lax.scan(lambda subtotal, share: (join(subtotal, share), None), head, tail)
    return subtotal


def total_of_pieces(array, axis):
    return lax.all_gather(array, axis).max(0)


def cut_along(array, dim, size):
    shape = array.shape
    tiles = array.reshape(*shape[:dim], size, shape[dim] // size, *shape[dim + 1 :])
    return jnp.moveaxis(tiles, dim, 0)


def sum_at_owner(array, axis, dim):
    tiles = cut_along(array, dim, lax.axis_size(axis))
    arrived = lax.all_to_all(tiles, axis, split_axis=0, concat_axis=0, tiled=True)
    return arrived.sum(axis=0)


def half_dist(first_set, second_set):
    cross_term = jnp.dot(
        first_set.T, second_set, precision=lax.Precision.HIGHEST, preferred_element_type=jnp.float32
    )
    first_sq = jnp.sum(first_set * first_set, axis=0)
    second_sq = jnp.sum(second_set * second_set, axis=0)
    return 0.5 * (first_sq[:, None] + second_sq[None, :]) - cross_term


def log_sum(values, along):
    top_val = jnp.max(values, axis=along, keepdims=True)
    return jnp.squeeze(top_val, along) + jnp.log(jnp.sum(jnp.exp(values - top_val), axis=along))


def combine_parts(earlier, latter):
    joined = jnp.maximum(earlier[0], latter[0])
    return (
        joined,
        earlier[1] * jnp.exp(earlier[0] - joined) + latter[1] * jnp.exp(latter[0] - joined),
    )


def on_device(src_pts, src_mass, tgt_pts, tgt_mass, listed, live):
    clusters = src_mass.shape[0]
    points = src_mass.shape[1]
    local_tgt = tgt_mass.shape[1]
    slot_count = listed.shape[2]
    src_total = jnp.sum(src_mass, axis=1)
    src_cent = jnp.sum(src_pts * src_mass[None], axis=2) / src_total[None]
    tgt_total = jnp.sum(tgt_mass, axis=0)
    tgt_cent = jnp.sum(tgt_pts * tgt_mass[None], axis=1) / tgt_total[None]
    all_cent, all_logb = (
        lax.all_gather(tgt_cent, "tgt", axis=1, tiled=True),
        lax.all_gather(jnp.log(tgt_total), "tgt", axis=0, tiled=True),
    )
    coarse_f = -EPS * log_sum(all_logb[None, :] - half_dist(src_cent, all_cent) / EPS, 1)
    src_logw = jnp.log(src_total)
    every_cent, every_logw, every_f = rows_first((src_cent, src_logw, coarse_f), "src", (1, 0, 0))
    coarse_terms = every_logw[:, None] + (every_f[:, None] - half_dist(every_cent, tgt_cent)) / EPS
    coarse_g = -EPS * log_sum(coarse_terms, 0)
    slot_ids = jnp.arange(slot_count, dtype=jnp.int32)
    chosen = listed[:, 0, :]
    alive_slot = slot_ids[None, :] < live[:, 0][:, None]

    def row_pass(cluster):
        columns = chosen[cluster]
        blocks = jnp.take(tgt_pts, columns, axis=2).reshape(3, -1)
        base_term = jnp.log(jnp.take(tgt_mass, columns, axis=1)) + coarse_g[columns][None, :] / EPS
        base_term = jnp.where(alive_slot[cluster][None, :], base_term, NEG).reshape(-1)
        cost_tile = half_dist(src_pts[:, cluster, :], blocks)
        scores = base_term[None, :] - cost_tile / EPS
        row_top = jnp.max(scores, axis=1)
        row_sum = jnp.sum(jnp.exp(scores - row_top[:, None]), axis=1)
        return (cost_tile, row_top, row_sum)

    cost_tiles, row_top, row_sum = lax.map(row_pass, jnp.arange(clusters, dtype=jnp.int32))
    row_top, row_sum = merged((row_top, row_sum), "tgt", combine_parts)
    fine_f = -EPS * (row_top + jnp.log(row_sum))
    src_logm = jnp.log(src_mass)

    def column_pass(packed):
        cost_tile, potential, log_mass = packed
        scores = log_mass[:, None] + (potential[:, None] - cost_tile) / EPS
        col_top = jnp.max(scores, axis=0)
        col_sum = jnp.sum(jnp.exp(scores - col_top[None, :]), axis=0)
        return (col_top.reshape(points, slot_count), col_sum.reshape(points, slot_count))

    col_top, col_sum = lax.map(column_pass, (cost_tiles, fine_f, src_logm))
    col_top = jnp.transpose(col_top, (1, 0, 2)).reshape(points, -1)
    col_sum = jnp.transpose(col_sum, (1, 0, 2)).reshape(points, -1)
    flat_ids = jnp.where(alive_slot, chosen, local_tgt).reshape(-1)
    top_local = jnp.full((points, local_tgt + 1), NEG, jnp.float32).at[:, flat_ids].max(col_top)
    sum_local = (
        jnp.zeros((points, local_tgt + 1), jnp.float32)
        .at[:, flat_ids]
        .add(col_sum * jnp.exp(col_top - top_local[:, flat_ids]))
    )
    top_local = top_local[:, :local_tgt]
    sum_local = sum_local[:, :local_tgt]
    share_rows = points // lax.axis_size("src")
    row_start = lax.axis_index("src") * share_rows
    top_all = total_of_pieces(top_local, "src")
    shifted = sum_local * jnp.exp(top_local - top_all)
    sum_mine = sum_at_owner(shifted, "src", 0)
    top_mine = lax.dynamic_slice_in_dim(top_all, row_start, share_rows, 0)
    fallback = (-coarse_g / EPS)[None, :]
    joined = jnp.maximum(top_mine, fallback)
    grand_total = sum_mine * jnp.exp(top_mine - joined) + jnp.exp(fallback - joined)
    fine_g = -EPS * (joined + jnp.log(grand_total))
    return (fine_f, fine_g)


def solution(mesh):
    placed = (
        P(None, "src", None),
        P("src", None),
        P(None, None, "tgt"),
        P(None, "tgt"),
        P("src", "tgt", None),
        P("src", "tgt"),
    )
    return jax.shard_map(
        on_device,
        mesh=mesh,
        in_specs=placed,
        out_specs=(P("src", None), P("src", "tgt")),
        check_vma=False,
    )
```

profile of v0, /device:TPU:1, one launch (start us, length us, event | category | flops | bytes accessed | tf_op | source)
XLA Modules:
  0.0 460.4 jit_solution(12193021447752270780)
XLA Ops:
  11.9 10.5 %all_gather.22 = f32[3,1024]{1,0:T(4,128)S(1)} all-gather(f32[3,256]{1,0:T(4,128)S(1)} %get-tuple-element.243), channel_id=1, replica_groups=mesh['src'=32,'tgt'=4] {'tgt'}, dimensions={1}, use_global_device_ids=true | all-gather | bytes 15360 | tf_op jit(solution)/shard_map/all_gather | solution.py:97
  22.4 7.4 %all-gather.2 = f32[4,1,256]{2,1,0:T(1,128)S(1)} all-gather(f32[1,1,256]{2,1,0:T(1,128)S(1)} %bitcast.156), channel_id=1, replica_groups=mesh['src'=32,'tgt'=4] {'tgt'}, dimensions={0}, use_global_device_ids=true | all-gather | bytes 5120 | tf_op jit(solution)/shard_map/all_gather | solution.py:98
  30.5 31.4 %all-gather.3 = f32[32,16,5]{1,2,0:T(8,128)S(1)} all-gather(f32[1,16,5]{1,2,0:T(8,128)S(1)} %maximum_bitcast_fusion), channel_id=1, replica_groups=mesh['src'=32,'tgt'=4] {'src'}, dimensions={0}, use_global_device_ids=true | all-gather | bytes 10560 | tf_op jit(solution)/shard_map/all_gather | solution.py:14
  64.3 211.8 %while.38 = (s32[]{:T(128)}, f32[16,256,2048]{2,1,0:T(8,128)}, f32[16,256]{1,0:T(8,128)}, f32[16,256]{1,0:T(8,128)}, s32[16]{0:T(128)S(1)}, /*index=5*/f32[3,16,...) while((s32[]{:T(128)}, f32[16,256,2048]{2,1,0:T(8,128)}, ...), condition=%wide.region_17.18_spmd, body=%wide.region_12.17_spmd.sunk | while | flops 24141652 | bytes 8773411 | solution.py:120
  69.0 3.5 bitcast_dynamic-update-slice_fusion.2
  82.2 3.4 bitcast_dynamic-update-slice_fusion.2
  95.4 3.5 bitcast_dynamic-update-slice_fusion.2
  108.7 3.5 bitcast_dynamic-update-slice_fusion.2
  121.9 3.5 bitcast_dynamic-update-slice_fusion.2
  135.2 3.4 bitcast_dynamic-update-slice_fusion.2
  148.4 3.5 bitcast_dynamic-update-slice_fusion.2
  161.7 3.5 bitcast_dynamic-update-slice_fusion.2
  174.9 3.5 bitcast_dynamic-update-slice_fusion.2
  188.2 3.4 bitcast_dynamic-update-slice_fusion.2
  201.4 3.5 bitcast_dynamic-update-slice_fusion.2
  214.6 3.5 bitcast_dynamic-update-slice_fusion.2
  227.9 3.5 bitcast_dynamic-update-slice_fusion.2
  241.2 3.4 bitcast_dynamic-update-slice_fusion.2
  254.4 3.5 bitcast_dynamic-update-slice_fusion.2
  267.6 3.5 bitcast_dynamic-update-slice_fusion.2
  276.9 9.1 %all-gather = f32[128,256]{1,0:T(8,128)S(1)} all-gather(f32[32,256]{1,0:T(8,128)S(1)} %pad_maximum_fusion), channel_id=2, replica_groups=mesh['src'=32,'tgt'=4] {'tgt'}, dimensions={0}, use_global_device_ids=true | all-gather | bytes 163840 | tf_op jit(solution)/shard_map/all_gather | solution.py:32
  286.3 91.3 %while.40 = (s32[]{:T(128)}, f32[16,256,8]{2,1,0:T(8,128)S(1)}, f32[16,256,8]{2,1,0:T(8,128)}, f32[16,256]{1,0:T(8,128)}, f32[16,256]{1,0:T(8,128)S(1)}, /*index=5*/f32[16,256,2048]{2,1,0:T(8,128)}, s32[]{:T(128)}) while((s32[]{:T(128)}, f32[16,256,8]{2,1,0:T(8,128)S(1)}, f32[16,256,8]{2,1,0:T(8,128)}, f32[16,256]{1,0:T(8,128)}, ...), condition=%wide.region_23.24_spmd, body=%wide.region_20.23_spmd.sunk | while | flops 4714498 | bytes 4784733 | solution.py:132
  289.0 2.2 exponential_reduce_fusion.7
  294.7 2.2 exponential_reduce_fusion.7
  300.4 2.2 exponential_reduce_fusion.7
  306.1 2.2 exponential_reduce_fusion.7
  311.8 2.2 exponential_reduce_fusion.7
  315.5 1.9 fusion.55
  317.5 2.2 exponential_reduce_fusion.7
  321.3 1.9 fusion.55
  323.2 2.2 exponential_reduce_fusion.7
  327.0 1.9 fusion.55
  328.9 2.2 exponential_reduce_fusion.7
  334.6 2.2 exponential_reduce_fusion.7
  340.3 2.2 exponential_reduce_fusion.7
  346.0 2.2 exponential_reduce_fusion.7
  349.8 1.9 fusion.55
  351.7 2.2 exponential_reduce_fusion.7
  357.4 2.2 exponential_reduce_fusion.7
  361.2 1.9 fusion.55
  363.1 2.2 exponential_reduce_fusion.7
  368.8 2.2 exponential_reduce_fusion.7
  374.5 2.2 exponential_reduce_fusion.7
  380.5 2.2 copy.63
  384.5 49.2 %all-gather.6.cloned.1.call-done = f32[8192,256]{1,0:T(8,128)} async-done(((f32[256,256]{1,0:T(8,128)}), f32[8192,256]{1,0:T(8,128)}) %all-gather.6.cloned.1.call-update) | async-done | bytes 8388624 | tf_op jit(solution)/shard_map/all_gather | solution.py:50
  433.7 4.0 reduce_max.47
  438.4 5.5 %all-to-all-start = ((f32[32,8,256]{2,1,0:T(8,128)}), f32[32,8,256]{2,1,0:T(8,128)S(1)}, u32[]{:S(2)}, u32[]{:S(2)}) async-start(f32[32,8,256]{2,1,0:T(8,128)} %multiply_bitcast_fusion), calls=%async_computation | async-start | bytes 524288 | tf_op jit(solution)/shard_map/all_to_all | solution.py:61
  443.9 9.0 %all-to-all-done = f32[32,8,256]{2,1,0:T(8,128)S(1)} async-done(((f32[32,8,256]{2,1,0:T(8,128)}), f32[32,8,256]{2,1,0:T(8,128)S(1)}, u32[]{:S(2)}, u32[]{:S(2)}) %all-to-all-start) | async-done | bytes 262176 | tf_op jit(solution)/shard_map/all_to_all | solution.py:61
  (719 shorter events, 184.8 us)
Async XLA Ops:
  7.2 55.4 %copy-start.1 = (f32[256,256]{1,0:T(8,128)S(1)}, f32[256,256]{1,0:T(8,128)}, u32[]{:S(2)}) copy-start(f32[256,256]{1,0:T(8,128)} %param.15) | copy-start | bytes 786436
  7.2 55.0 %copy-start = (f32[3,256,256]{2,1,0:T(8,128)S(1)}, f32[3,256,256]{2,1,0:T(8,128)}, u32[]{:S(2)}) copy-start(f32[3,256,256]{2,1,0:T(8,128)} %param.14) | copy-start | bytes 2359300
  7.2 426.5 %all-gather.6.cloned.1.call-start = ((), (), s32[]{:S(2)}) async-start(), calls=%async_computation.1 | async-start | bytes 8650752 | tf_op jit(solution)/shard_map/all_gather | solution.py:50
  64.3 8.2 %copy-start.7 = (s32[16,8]{1,0:T(8,128)}, s32[16,8]{1,0:T(8,128)S(1)}, u32[]{:S(2)}) copy-start(s32[16,8]{1,0:T(8,128)S(1)} %get-tuple-element.449) | copy-start | bytes 1540 | tf_op jit(solution)/shard_map/while
  64.3 8.2 %copy-start.11 = (s32[16]{0:T(128)}, s32[16]{0:T(128)S(1)}, u32[]{:S(2)}) copy-start(s32[16]{0:T(128)S(1)} %get-tuple-element.447) | copy-start | bytes 196 | tf_op jit(solution)/shard_map/while
  64.3 9.4 %copy-start.5 = (pred[16,8]{1,0:T(8,128)(4,1)}, pred[16,8]{1,0:T(8,128)(4,1)S(1)}, u32[]{:S(2)}) copy-start(pred[16,8]{1,0:T(8,128)(4,1)S(1)} %get-tuple-element.451) | copy-start | bytes 388 | tf_op jit(solution)/shard_map/while
  77.5 9.3 %copy-start.5 = (pred[16,8]{1,0:T(8,128)(4,1)}, pred[16,8]{1,0:T(8,128)(4,1)S(1)}, u32[]{:S(2)}) copy-start(pred[16,8]{1,0:T(8,128)(4,1)S(1)} %get-tuple-element.451) | copy-start | bytes 388 | tf_op jit(solution)/shard_map/while
  90.7 8.2 %copy-start.7 = (s32[16,8]{1,0:T(8,128)}, s32[16,8]{1,0:T(8,128)S(1)}, u32[]{:S(2)}) copy-start(s32[16,8]{1,0:T(8,128)S(1)} %get-tuple-element.449) | copy-start | bytes 1540 | tf_op jit(solution)/shard_map/while
  90.7 8.2 %copy-start.11 = (s32[16]{0:T(128)}, s32[16]{0:T(128)S(1)}, u32[]{:S(2)}) copy-start(s32[16]{0:T(128)S(1)} %get-tuple-element.447) | copy-start | bytes 196 | tf_op jit(solution)/shard_map/while
  90.7 9.4 %copy-start.5 = (pred[16,8]{1,0:T(8,128)(4,1)}, pred[16,8]{1,0:T(8,128)(4,1)S(1)}, u32[]{:S(2)}) copy-start(pred[16,8]{1,0:T(8,128)(4,1)S(1)} %get-tuple-element.451) | copy-start | bytes 388 | tf_op jit(solution)/shard_map/while
  104.0 8.2 %copy-start.7 = (s32[16,8]{1,0:T(8,128)}, s32[16,8]{1,0:T(8,128)S(1)}, u32[]{:S(2)}) copy-start(s32[16,8]{1,0:T(8,128)S(1)} %get-tuple-element.449) | copy-start | bytes 1540 | tf_op jit(solution)/shard_map/while
  104.0 8.2 %copy-start.11 = (s32[16]{0:T(128)}, s32[16]{0:T(128)S(1)}, u32[]{:S(2)}) copy-start(s32[16]{0:T(128)S(1)} %get-tuple-element.447) | copy-start | bytes 196 | tf_op jit(solution)/shard_map/while
  104.0 9.4 %copy-start.5 = (pred[16,8]{1,0:T(8,128)(4,1)}, pred[16,8]{1,0:T(8,128)(4,1)S(1)}, u32[]{:S(2)}) copy-start(pred[16,8]{1,0:T(8,128)(4,1)S(1)} %get-tuple-element.451) | copy-start | bytes 388 | tf_op jit(solution)/shard_map/while
  117.2 8.2 %copy-start.7 = (s32[16,8]{1,0:T(8,128)}, s32[16,8]{1,0:T(8,128)S(1)}, u32[]{:S(2)}) copy-start(s32[16,8]{1,0:T(8,128)S(1)} %get-tuple-element.449) | copy-start | bytes 1540 | tf_op jit(solution)/shard_map/while
  117.2 8.2 %copy-start.11 = (s32[16]{0:T(128)}, s32[16]{0:T(128)S(1)}, u32[]{:S(2)}) copy-start(s32[16]{0:T(128)S(1)} %get-tuple-element.447) | copy-start | bytes 196 | tf_op jit(solution)/shard_map/while
  117.2 9.4 %copy-start.5 = (pred[16,8]{1,0:T(8,128)(4,1)}, pred[16,8]{1,0:T(8,128)(4,1)S(1)}, u32[]{:S(2)}) copy-start(pred[16,8]{1,0:T(8,128)(4,1)S(1)} %get-tuple-element.451) | copy-start | bytes 388 | tf_op jit(solution)/shard_map/while
  130.5 8.1 %copy-start.7 = (s32[16,8]{1,0:T(8,128)}, s32[16,8]{1,0:T(8,128)S(1)}, u32[]{:S(2)}) copy-start(s32[16,8]{1,0:T(8,128)S(1)} %get-tuple-element.449) | copy-start | bytes 1540 | tf_op jit(solution)/shard_map/while
  130.5 9.3 %copy-start.5 = (pred[16,8]{1,0:T(8,128)(4,1)}, pred[16,8]{1,0:T(8,128)(4,1)S(1)}, u32[]{:S(2)}) copy-start(pred[16,8]{1,0:T(8,128)(4,1)S(1)} %get-tuple-element.451) | copy-start | bytes 388 | tf_op jit(solution)/shard_map/while
  143.7 8.2 %copy-start.7 = (s32[16,8]{1,0:T(8,128)}, s32[16,8]{1,0:T(8,128)S(1)}, u32[]{:S(2)}) copy-start(s32[16,8]{1,0:T(8,128)S(1)} %get-tuple-element.449) | copy-start | bytes 1540 | tf_op jit(solution)/shard_map/while
  143.7 8.2 %copy-start.11 = (s32[16]{0:T(128)}, s32[16]{0:T(128)S(1)}, u32[]{:S(2)}) copy-start(s32[16]{0:T(128)S(1)} %get-tuple-element.447) | copy-start | bytes 196 | tf_op jit(solution)/shard_map/while
  143.7 9.4 %copy-start.5 = (pred[16,8]{1,0:T(8,128)(4,1)}, pred[16,8]{1,0:T(8,128)(4,1)S(1)}, u32[]{:S(2)}) copy-start(pred[16,8]{1,0:T(8,128)(4,1)S(1)} %get-tuple-element.451) | copy-start | bytes 388 | tf_op jit(solution)/shard_map/while
  157.0 8.2 %copy-start.7 = (s32[16,8]{1,0:T(8,128)}, s32[16,8]{1,0:T(8,128)S(1)}, u32[]{:S(2)}) copy-start(s32[16,8]{1,0:T(8,128)S(1)} %get-tuple-element.449) | copy-start | bytes 1540 | tf_op jit(solution)/shard_map/while
  157.0 8.2 %copy-start.11 = (s32[16]{0:T(128)}, s32[16]{0:T(128)S(1)}, u32[]{:S(2)}) copy-start(s32[16]{0:T(128)S(1)} %get-tuple-element.447) | copy-start | bytes 196 | tf_op jit(solution)/shard_map/while
  157.0 9.4 %copy-start.5 = (pred[16,8]{1,0:T(8,128)(4,1)}, pred[16,8]{1,0:T(8,128)(4,1)S(1)}, u32[]{:S(2)}) copy-start(pred[16,8]{1,0:T(8,128)(4,1)S(1)} %get-tuple-element.451) | copy-start | bytes 388 | tf_op jit(solution)/shard_map/while
  170.2 8.2 %copy-start.7 = (s32[16,8]{1,0:T(8,128)}, s32[16,8]{1,0:T(8,128)S(1)}, u32[]{:S(2)}) copy-start(s32[16,8]{1,0:T(8,128)S(1)} %get-tuple-element.449) | copy-start | bytes 1540 | tf_op jit(solution)/shard_map/while
  170.2 8.2 %copy-start.11 = (s32[16]{0:T(128)}, s32[16]{0:T(128)S(1)}, u32[]{:S(2)}) copy-start(s32[16]{0:T(128)S(1)} %get-tuple-element.447) | copy-start | bytes 196 | tf_op jit(solution)/shard_map/while
  170.2 9.4 %copy-start.5 = (pred[16,8]{1,0:T(8,128)(4,1)}, pred[16,8]{1,0:T(8,128)(4,1)S(1)}, u32[]{:S(2)}) copy-start(pred[16,8]{1,0:T(8,128)(4,1)S(1)} %get-tuple-element.451) | copy-start | bytes 388 | tf_op jit(solution)/shard_map/while
  183.5 8.1 %copy-start.7 = (s32[16,8]{1,0:T(8,128)}, s32[16,8]{1,0:T(8,128)S(1)}, u32[]{:S(2)}) copy-start(s32[16,8]{1,0:T(8,128)S(1)} %get-tuple-element.449) | copy-start | bytes 1540 | tf_op jit(solution)/shard_map/while
  183.5 9.3 %copy-start.5 = (pred[16,8]{1,0:T(8,128)(4,1)}, pred[16,8]{1,0:T(8,128)(4,1)S(1)}, u32[]{:S(2)}) copy-start(pred[16,8]{1,0:T(8,128)(4,1)S(1)} %get-tuple-element.451) | copy-start | bytes 388 | tf_op jit(solution)/shard_map/while
  196.7 8.2 %copy-start.7 = (s32[16,8]{1,0:T(8,128)}, s32[16,8]{1,0:T(8,128)S(1)}, u32[]{:S(2)}) copy-start(s32[16,8]{1,0:T(8,128)S(1)} %get-tuple-element.449) | copy-start | bytes 1540 | tf_op jit(solution)/shard_map/while
  196.7 8.2 %copy-start.11 = (s32[16]{0:T(128)}, s32[16]{0:T(128)S(1)}, u32[]{:S(2)}) copy-start(s32[16]{0:T(128)S(1)} %get-tuple-element.447) | copy-start | bytes 196 | tf_op jit(solution)/shard_map/while
  196.7 9.4 %copy-start.5 = (pred[16,8]{1,0:T(8,128)(4,1)}, pred[16,8]{1,0:T(8,128)(4,1)S(1)}, u32[]{:S(2)}) copy-start(pred[16,8]{1,0:T(8,128)(4,1)S(1)} %get-tuple-element.451) | copy-start | bytes 388 | tf_op jit(solution)/shard_map/while
  209.9 8.2 %copy-start.7 = (s32[16,8]{1,0:T(8,128)}, s32[16,8]{1,0:T(8,128)S(1)}, u32[]{:S(2)}) copy-start(s32[16,8]{1,0:T(8,128)S(1)} %get-tuple-element.449) | copy-start | bytes 1540 | tf_op jit(solution)/shard_map/while
  209.9 8.2 %copy-start.11 = (s32[16]{0:T(128)}, s32[16]{0:T(128)S(1)}, u32[]{:S(2)}) copy-start(s32[16]{0:T(128)S(1)} %get-tuple-element.447) | copy-start | bytes 196 | tf_op jit(solution)/shard_map/while
  209.9 9.4 %copy-start.5 = (pred[16,8]{1,0:T(8,128)(4,1)}, pred[16,8]{1,0:T(8,128)(4,1)S(1)}, u32[]{:S(2)}) copy-start(pred[16,8]{1,0:T(8,128)(4,1)S(1)} %get-tuple-element.451) | copy-start | bytes 388 | tf_op jit(solution)/shard_map/while
  223.2 8.2 %copy-start.7 = (s32[16,8]{1,0:T(8,128)}, s32[16,8]{1,0:T(8,128)S(1)}, u32[]{:S(2)}) copy-start(s32[16,8]{1,0:T(8,128)S(1)} %get-tuple-element.449) | copy-start | bytes 1540 | tf_op jit(solution)/shard_map/while
  223.2 8.2 %copy-start.11 = (s32[16]{0:T(128)}, s32[16]{0:T(128)S(1)}, u32[]{:S(2)}) copy-start(s32[16]{0:T(128)S(1)} %get-tuple-element.447) | copy-start | bytes 196 | tf_op jit(solution)/shard_map/while
  223.2 9.4 %copy-start.5 = (pred[16,8]{1,0:T(8,128)(4,1)}, pred[16,8]{1,0:T(8,128)(4,1)S(1)}, u32[]{:S(2)}) copy-start(pred[16,8]{1,0:T(8,128)(4,1)S(1)} %get-tuple-element.451) | copy-start | bytes 388 | tf_op jit(solution)/shard_map/while
  236.5 8.1 %copy-start.7 = (s32[16,8]{1,0:T(8,128)}, s32[16,8]{1,0:T(8,128)S(1)}, u32[]{:S(2)}) copy-start(s32[16,8]{1,0:T(8,128)S(1)} %get-tuple-element.449) | copy-start | bytes 1540 | tf_op jit(solution)/shard_map/while
  236.5 9.3 %copy-start.5 = (pred[16,8]{1,0:T(8,128)(4,1)}, pred[16,8]{1,0:T(8,128)(4,1)S(1)}, u32[]{:S(2)}) copy-start(pred[16,8]{1,0:T(8,128)(4,1)S(1)} %get-tuple-element.451) | copy-start | bytes 388 | tf_op jit(solution)/shard_map/while
  249.7 8.2 %copy-start.7 = (s32[16,8]{1,0:T(8,128)}, s32[16,8]{1,0:T(8,128)S(1)}, u32[]{:S(2)}) copy-start(s32[16,8]{1,0:T(8,128)S(1)} %get-tuple-element.449) | copy-start | bytes 1540 | tf_op jit(solution)/shard_map/while
  249.7 8.2 %copy-start.11 = (s32[16]{0:T(128)}, s32[16]{0:T(128)S(1)}, u32[]{:S(2)}) copy-start(s32[16]{0:T(128)S(1)} %get-tuple-element.447) | copy-start | bytes 196 | tf_op jit(solution)/shard_map/while
  249.7 9.4 %copy-start.5 = (pred[16,8]{1,0:T(8,128)(4,1)}, pred[16,8]{1,0:T(8,128)(4,1)S(1)}, u32[]{:S(2)}) copy-start(pred[16,8]{1,0:T(8,128)(4,1)S(1)} %get-tuple-element.451) | copy-start | bytes 388 | tf_op jit(solution)/shard_map/while
  262.9 8.2 %copy-start.7 = (s32[16,8]{1,0:T(8,128)}, s32[16,8]{1,0:T(8,128)S(1)}, u32[]{:S(2)}) copy-start(s32[16,8]{1,0:T(8,128)S(1)} %get-tuple-element.449) | copy-start | bytes 1540 | tf_op jit(solution)/shard_map/while
  262.9 8.2 %copy-start.11 = (s32[16]{0:T(128)}, s32[16]{0:T(128)S(1)}, u32[]{:S(2)}) copy-start(s32[16]{0:T(128)S(1)} %get-tuple-element.447) | copy-start | bytes 196 | tf_op jit(solution)/shard_map/while
  262.9 9.4 %copy-start.5 = (pred[16,8]{1,0:T(8,128)(4,1)}, pred[16,8]{1,0:T(8,128)(4,1)S(1)}, u32[]{:S(2)}) copy-start(pred[16,8]{1,0:T(8,128)(4,1)S(1)} %get-tuple-element.451) | copy-start | bytes 388 | tf_op jit(solution)/shard_map/while
  433.7 19.2 %copy-start.9 = (f32[256]{0:T(256)S(1)}, f32[256]{0:T(256)}, u32[]{:S(2)}) copy-start(f32[256]{0:T(256)} %get-tuple-element.240) | copy-start | bytes 3076
  438.4 14.5 %all-to-all-start = ((f32[32,8,256]{2,1,0:T(8,128)}), f32[32,8,256]{2,1,0:T(8,128)S(1)}, u32[]{:S(2)}, u32[]{:S(2)}) async-start(f32[32,8,256]{2,1,0:T(8,128)} %multiply_bitcast_fusion), calls=%async_computation | async-start | bytes 524288 | tf_op jit(solution)/shard_map/all_to_all | solution.py:61
  (57 other events, 219.9 us)
Sparse Core Ops, SparseCore 0:
  380.6 53.0 all-gather.5
where the time goes:
time: 465 us; the launch traced here: 460 us
  local copies, waits for them, and re-layouts  137 us (29%)
  other arithmetic  97.3 us (21%)
  blocking collectives  58.5 us (13%)
  waiting for transfers between devices  58.2 us (13%)
  matrix products  56.7 us (12%)
  loops' own time  33.4 us (7%)
  between operations  14.3 us (3%)
  starting transfers between devices  5.52 us (1%)
    dot_general x18, matrix products, half_dist(): jnp.dot(first_set.T, second_set, precision=lax.Precision.HIGHEST, preferr...  56.7 us
    all_gather x1, waiting for transfers between devices, total_of_pieces(): return lax.all_gather(array, axis).max(0)  49.2 us
    dynamic_update_slice x32, local copies, waits for them, and re-layouts, on_device(): lax.map(row_pass, jnp.arange(clusters, dtype=jnp.int32))  41.7 us
    reduce_sum x16, other arithmetic, column_pass(): col_sum = jnp.sum(jnp.exp(scores - col_top[None, :]), axis=0)  34.5 us
    another operation x1, loops' own time, on_device(): lax.map(row_pass, jnp.arange(clusters, dtype=jnp.int32))  32.8 us
    all_gather x1, blocking collectives, rows_first(): whole = lax.all_gather(both, axis, axis=0, tiled=True)  31.4 us
    reduce_max x16, other arithmetic, column_pass(): col_top = jnp.max(scores, axis=0)  31 us
    dynamic_slice x16, local copies, waits for them, and re-layouts, row_pass(): cost_tile = half_dist(src_pts[:, cluster, :], blocks)  12 us
  transfers between devices with their start and end apart: 2, of which 2 were waited for; matrix products, arithmetic and copies ran while one was open for 1% of the time, Pallas kernels for 0%

commit v1 on v0

v1 whole, which is shorter than its diff:
```python
import functools
import math

import jax
import jax.numpy as jnp
from jax import lax
from jax.experimental import pallas as pl
from jax.experimental.pallas import tpu as pltpu
from jax.sharding import PartitionSpec as P

EPS = 0.1
NEG = -1e30
ALPHA = math.log2(math.e) / EPS
UNSCALE = EPS * math.log(2.0)
F32 = jnp.float32
VMEM = pl.BlockSpec(memory_space=pltpu.VMEM)
SMEM = pl.BlockSpec(memory_space=pltpu.SMEM)
ANY = pl.BlockSpec(memory_space=pl.ANY)


def lane_iota(shape):
    return lax.broadcasted_iota(jnp.int32, shape, len(shape) - 1)


def centroid_kernel(pos, sp, sm, tp, tm, row_out, own_out):
    s, t = pos[0], pos[1]
    mass = sm[...]
    total = jnp.sum(mass, axis=1, keepdims=True)
    inv = 1.0 / total
    cols = [jnp.sum(sp[d] * mass, axis=1, keepdims=True) * inv for d in range(3)]
    cols.append(jnp.log2(total))
    lane = lane_iota((mass.shape[0], 128))
    z = jnp.zeros((mass.shape[0], 128), F32)
    for q in range(4):
        z = jnp.where(lane == q, cols[q], z)
    zt = jnp.concatenate([z, jnp.zeros((128 - mass.shape[0], 128), F32)], axis=0).T
    lane = lane_iota((1, 128))
    row = jnp.zeros((1, 128), F32)
    for q in range(4):
        piece = pltpu.roll(zt[q : q + 1, :], lax.rem(128 - 4 * t, 128), 1)
        row = row + pltpu.roll(jnp.where(lane < 4, piece, 0.0), 4 * q, 1)
    weight = tm[...]
    total = jnp.sum(weight, axis=0, keepdims=True)
    inv = 1.0 / total
    rows = [jnp.sum(tp[d] * weight, axis=0, keepdims=True) * inv for d in range(3)]
    rows.append(jnp.log2(total))
    for q in range(4):
        own_out[q : q + 1, :] = rows[q]
        half = jnp.where(s >= 16, rows[q][:, 128:], rows[q][:, :128])
        piece = pltpu.roll(half, lax.rem(128 - 8 * lax.rem(s, 16), 128), 1)
        row = row + pltpu.roll(jnp.where(lane < 8, piece, 0.0), 16 + 8 * q, 1)
    row_out[...] = jnp.broadcast_to(row, row_out.shape)


def row_kernel(listed, live, sp, tp, tm, alive, e_out, m_out, r_out, yt, xc, mcol, scol, ebuf, sems):
    clusters, slots = 16, 8
    y = [tp[d] for d in range(3)]
    base = jnp.log2(tm[...]) - (0.5 * ALPHA) * (y[0] * y[0] + y[1] * y[1] + y[2] * y[2])
    for d in range(3):
        yt[d] = y[d].T
    yt[3] = base.T
    lane = lane_iota((16, 128))

    def flush(b, slot):
        return pltpu.make_async_copy(ebuf.at[slot], e_out.at[b], sems.at[slot])

    def cluster(c, count):
        for d in range(3):
            line = sp[d, pl.ds(c, 1), :] * ALPHA
            xc[d] = jnp.broadcast_to(line, (128, 256)).T

        def block(k, count):
            b = c * slots + k
            slot = lax.rem(count, 2)

            @pl.when(count >= 2)
            def _():
                flush(b, slot).wait()

            at = listed[b]
            rows = [yt[q, pl.ds(at, 1), :] for q in range(4)]
            for i in range(0, 256, 16):
                xs = [xc[d, i : i + 16, :] for d in range(3)]
                halves = []
                for h in (0, 128):
                    v = rows[3][:, h : h + 128] + xs[0] * rows[0][:, h : h + 128]
                    v = v + xs[1] * rows[1][:, h : h + 128]
                    halves.append(v + xs[2] * rows[2][:, h : h + 128])
                top = jnp.max(jnp.maximum(*halves), axis=1, keepdims=True)
                es = [jnp.exp2(v - top) for v in halves]
                total = jnp.sum(es[0] + es[1], axis=1, keepdims=True)
                for h in range(2):
                    ebuf[slot, i : i + 16, 128 * h : 128 * h + 128] = es[h].astype(jnp.bfloat16)
                mcol[i : i + 16, :] = jnp.where(lane == b, top, mcol[i : i + 16, :])
                scol[i : i + 16, :] = jnp.where(lane == b, total, scol[i : i + 16, :])
            flush(b, slot).start()
            return count + 1

        return lax.fori_loop(0, live[c], block, count)

    count = lax.fori_loop(0, clusters, cluster, 0)
    flush(0, lax.rem(count, 2)).wait()
    flush(0, lax.rem(count + 1, 2)).wait()
    xn = (-0.5 * ALPHA) * (sp[0] * sp[0] + sp[1] * sp[1] + sp[2] * sp[2])
    ok = alive[...] > 0
    m = jnp.where(ok, mcol[...].T, 0.0).reshape(clusters, slots, 256) + xn[:, None, :]
    m = m.reshape(clusters * slots, 256)
    m_out[...] = m
    r_out[...] = jnp.where(ok, m + jnp.log2(jnp.where(ok, scol[...].T, 1.0)), NEG)


def log2_sum(parts, axis):
    top = functools.reduce(jnp.maximum, [jnp.max(p, axis=axis, keepdims=True) for p in parts])
    total = sum(jnp.sum(jnp.exp2(p - top), axis=axis, keepdims=True) for p in parts)
    return top + jnp.log2(total)


def coarse_kernel(got, own, m_in, r_in, listed, g_out, mg_out, l_out):
    table = got[...]
    turned = table.T
    tgt = [[turned[16 + 8 * q + li : 17 + 8 * q + li, :] for q in range(4)] for li in range(8)]
    src = [[table[:, 4 * q + ci : 4 * q + ci + 1] for q in range(4)] for ci in range(4)]

    def score(x, y):
        gap = [x[d] - y[d] for d in range(3)]
        return (-0.5 * ALPHA) * (gap[0] * gap[0] + gap[1] * gap[1] + gap[2] * gap[2])

    mine = [own[q : q + 1, :] for q in range(4)]
    terms = []
    for x in src:
        f = -log2_sum([score(x, y) + y[3] for y in tgt], 1)
        terms.append(score(x, mine) + (x[3] + f))
    g = -log2_sum(terms, 0)
    g_out[...] = jnp.broadcast_to(g, g_out.shape)
    slots = listed.shape[0]
    hit = lane_iota((slots, 256)) == listed[...]
    picked = jnp.sum(jnp.where(hit, g, 0.0), axis=1, keepdims=True)
    mg_out[...] = m_in[...] + picked
    r = (r_in[...] + picked).reshape(16, 8, 256)
    l_out[...] = log2_sum([r], 1).reshape(16, 256)


def column_kernel(listed, live, sm, mg, l0, l1, l2, l3, e_in, f_out, s_out, w, st, ebuf, sems):
    clusters, slots = 16, 8
    f = -log2_sum([p[...][None] for p in (l0, l1, l2, l3)], 0)[0]
    f_out[...] = f * UNSCALE
    weights = sm[...][:, None, :] * jnp.exp2(mg[...].reshape(clusters, slots, 256) + f[:, None, :])
    high = weights.astype(jnp.bfloat16).astype(F32)
    w[...] = jnp.concatenate([high, weights - high], axis=1).astype(jnp.bfloat16)
    st[...] = jnp.zeros_like(st)

    def fetch(b, side, k):
        return pltpu.make_async_copy(e_in.at[b], ebuf.at[side, k], sems.at[side, k])

    def start(c, side):
        def one(k, _):
            fetch(c * slots + k, side, k).start()
            return 0

        lax.fori_loop(0, live[c], one, 0)

    start(0, 0)
    sub = lax.broadcasted_iota(jnp.int32, (2 * slots, 256), 0)

    def cluster(c, _):
        side = lax.rem(c, 2)

        @pl.when(c + 1 < clusters)
        def _():
            start(c + 1, 1 - side)

        lhs = w[c]

        def block(k, _):
            fetch(c * slots + k, side, k).wait()
            out = jnp.dot(lhs, ebuf[side, k], preferred_element_type=F32)
            out = jnp.sum(jnp.where((sub & 7) == k, out, 0.0), axis=0, keepdims=True)
            at = listed[c * slots + k]
            st[pl.ds(at, 1), :] = st[pl.ds(at, 1), :] + out
            return 0

        return lax.fori_loop(0, live[c], block, 0)

    lax.fori_loop(0, clusters, cluster, 0)
    s_out[...] = st[...].T.reshape(32, 8, 256)


def on_device(src_pts, src_mass, tgt_pts, tgt_mass, listed, live):
    shape = jax.ShapeDtypeStruct
    s, t = lax.axis_index("src"), lax.axis_index("tgt")
    pos = jnp.stack([s, t]).astype(jnp.int32)
    row, own = pl.pallas_call(
        centroid_kernel,
        out_shape=(shape((128, 128), F32), shape((8, 256), F32)),
        in_specs=[SMEM, VMEM, VMEM, VMEM, VMEM],
        out_specs=(VMEM, VMEM),
        name="centroids",
    )(pos, src_pts, src_mass, tgt_pts, tgt_mass)
    got = lax.all_to_all(row, ("src", "tgt"), split_axis=0, concat_axis=0, tiled=True)
    flat = listed.reshape(128)
    counts = live.reshape(16)
    column = listed.reshape(128, 1)
    alive = (jnp.arange(8, dtype=jnp.int32)[None, :] < counts[:, None]).astype(jnp.int32).reshape(128, 1)
    e, m, r = pl.pallas_call(
        row_kernel,
        out_shape=(shape((128, 256, 256), jnp.bfloat16), shape((128, 256), F32), shape((128, 256), F32)),
        in_specs=[SMEM, SMEM, VMEM, VMEM, VMEM, VMEM],
        out_specs=(ANY, VMEM, VMEM),
        scratch_shapes=[
            pltpu.VMEM((4, 256, 256), F32),
            pltpu.VMEM((3, 256, 128), F32),
            pltpu.VMEM((256, 128), F32),
            pltpu.VMEM((256, 128), F32),
            pltpu.VMEM((2, 256, 256), jnp.bfloat16),
            pltpu.SemaphoreType.DMA((2,)),
        ],
        cost_estimate=pl.CostEstimate(flops=100_000_000, bytes_accessed=10_000_000, transcendentals=5_000_000),
        name="rows",
    )(flat, counts, src_pts, tgt_pts, tgt_mass, alive)
    g, mg, part = pl.pallas_call(
        coarse_kernel,
        out_shape=(shape((8, 256), F32), shape((128, 256), F32), shape((16, 256), F32)),
        in_specs=[VMEM] * 5,
        out_specs=(VMEM, VMEM, VMEM),
        name="coarse",
    )(got, own, m, r, column)
    parts = [part] + [
        lax.ppermute(part, "tgt", [(i, (i + k) % 4) for i in range(4)]) for k in (1, 2, 3)
    ]
    fine_f, sums = pl.pallas_call(
        column_kernel,
        out_shape=(shape((16, 256), F32), shape((32, 8, 256), F32)),
        in_specs=[SMEM, SMEM] + [VMEM] * 6 + [ANY],
        out_specs=(VMEM, VMEM),
        scratch_shapes=[
            pltpu.VMEM((16, 16, 256), jnp.bfloat16),
            pltpu.VMEM((256, 256), F32),
            pltpu.VMEM((2, 8, 256, 256), jnp.bfloat16),
            pltpu.SemaphoreType.DMA((2, 8)),
        ],
        name="columns",
    )(flat, counts, src_mass, mg, *parts, e)
    arrived = lax.all_to_all(sums, "src", split_axis=0, concat_axis=0, tiled=True)
    mass = lax.dynamic_slice_in_dim(tgt_mass, s * 8, 8, 0)
    fine_g = (g - jnp.log2(1.0 + arrived.sum(axis=0) / mass)) * UNSCALE
    return fine_f, fine_g


def solution(mesh):
    placed = (
        P(None, "src", None),
        P("src", None),
        P(None, None, "tgt"),
        P(None, "tgt"),
        P("src", "tgt", None),
        P("src", "tgt"),
    )
    return jax.shard_map(
        on_device,
        mesh=mesh,
        in_specs=placed,
        out_specs=(P("src", None), P("src", "tgt")),
        check_vma=False,
    )
```

time: 465 us -> 108 us (0.23)
  local copies, waits for them, and re-layouts: 137 us -> 4.04 us
  other arithmetic: 97.3 us -> 2.67 us
  blocking collectives: 58.5 us -> 0 us
  matrix products: 56.7 us -> 0 us
  Pallas kernels: 0 us -> 49.4 us
  waiting for transfers between devices: 58.2 us -> 12.1 us
  loops' own time: 33.4 us -> 0 us
  starting transfers between devices: 5.52 us -> 38.7 us
  between operations: 14.3 us -> 0.71 us
    all_gather x4 -> x0, blocking collectives: 58.5 us -> none  [the longest x1 31.4 us: rows_first(): whole = lax.all_gather(both, axis, axis=0, tiled=True)]
    dot_general x18 -> x0, matrix products: 56.7 us -> none  [half_dist(): jnp.dot(first_set.T, second_set, precision=lax.Precision.HIGHEST, preferr...]
    dynamic_update_slice x48 -> x0, local copies, waits for them, and re-layouts: 52.4 us -> none  [the longest x32 41.7 us: on_device(): lax.map(row_pass, jnp.arange(clusters, dtype=jnp.int32))]
    pallas_call x0 -> x4, Pallas kernels: none -> 49.4 us  [the longest x1 26.4 us: on_device(): pl.pallas_call(row_kernel, out_shape=(shape((128, 256, 256), jnp.bfloat16...]
    all_gather x1 -> x0, waiting for transfers between devices: 49.2 us -> none  [total_of_pieces(): return lax.all_gather(array, axis).max(0)]
    reduce_sum x73 -> x1, other arithmetic: 48.5 us -> 0.04 us  [on_device(): fine_g = (g - jnp.log2(1.0 + arrived.sum(axis=0) / mass)) * UNSCALE]
    reduce_max x33 -> x0, other arithmetic: 39.6 us -> none  [the longest x16 31 us: column_pass(): col_top = jnp.max(scores, axis=0)]
    another operation x3 -> x0, loops' own time: 33.4 us -> none  [the longest x1 32.8 us: on_device(): lax.map(row_pass, jnp.arange(clusters, dtype=jnp.int32))]
  transfers between devices with their start and end apart: 2 -> 5, of which waited for: 2 -> 3; matrix products, arithmetic and copies ran while one was open for 1% -> 3% of each run, Pallas kernels for 0% -> 25%
where the time goes in v1:
time: 108 us
  Pallas kernels  49.4 us (46%)
  starting transfers between devices  38.7 us (36%)
  waiting for transfers between devices  12.1 us (11%)
  local copies, waits for them, and re-layouts  4.04 us (4%)
  other arithmetic  2.67 us (2%)
    pallas_call x1, Pallas kernels, on_device(): pl.pallas_call(row_kernel, out_shape=(shape((128, 256, 256), jnp.bfloat16...  26.4 us
    all_to_all x1, starting transfers between devices, on_device(): lax.all_to_all(sums, 'src', split_axis=0, concat_axis=0, tiled=True)  17.6 us
    pallas_call x1, Pallas kernels, on_device(): pl.pallas_call(column_kernel, out_shape=(shape((16, 256), F32), shape((32...  16.5 us
    all_to_all x1, starting transfers between devices, on_device(): lax.all_to_all(row, ('src', 'tgt'), split_axis=0, concat_axis=0, tiled=True)  11.5 us
    ppermute x3, starting transfers between devices, on_device(): lax.ppermute(part, 'tgt', [(i, (i + k) % 4) for i in range(4)])  9.62 us
    all_to_all x1, waiting for transfers between devices, on_device(): lax.all_to_all(sums, 'src', split_axis=0, concat_axis=0, tiled=True)  8.96 us
    pallas_call x1, Pallas kernels, on_device(): pl.pallas_call(coarse_kernel, out_shape=(shape((8, 256), F32), shape((128...  4.31 us
    ppermute x3, waiting for transfers between devices, on_device(): lax.ppermute(part, 'tgt', [(i, (i + k) % 4) for i in range(4)])  3.17 us
  transfers between devices with their start and end apart: 5, of which 3 were waited for; matrix products, arithmetic and copies ran while one was open for 3% of the time, Pallas kernels for 25%

profile of v1, /device:TPU:1, one launch (start us, length us, event | category | flops | bytes accessed | tf_op | source)
XLA Modules:
  0.0 107.6 jit_solution(17328181086283404977)
XLA Ops:
  0.6 0.6 pad_add_fusion.pos
  1.2 2.2 %centroids.1 = (f32[128,128]{1,0:T(8,128)}, f32[8,256]{1,0:T(8,128)}) custom-call(s32[2]{0:T(128)} %pad_add_fusion.pos, f32[3,16,256]{2,1,0:T(8,128)} %sp.3, f32[16,256]{1,0:T(8,128)} %sm.3, f32[3,256,256]{2,1,0:T(8,128)} %tp.3, f32[256,256]{1,0:T(8,128)} %tm.3), custom_call_target="tpu_custom_call" | custom-call | tf_op jit(solution)/shard_map/centroids/pallas_call | solution.py:192
  3.4 11.5 %all-to-all-start = ((f32[128,1,128]{2,1,0:T(1,128)}), f32[128,1,128]{2,1,0:T(1,128)S(1)}, u32[]{:S(2)}, u32[]{:S(2)}) async-start(f32[128,1,128]{2,1,0:T(1,128)} %bitcast.12), calls=%async_computation | async-start | bytes 131072 | tf_op jit(solution)/shard_map/all_to_all | solution.py:199
  14.9 0.7 fusion
  15.6 0.8 copy.16
  16.4 0.7 reshape.43.listed
  17.0 0.7 reshape.48.listed
  17.7 0.7 reshape.47.alive
  18.4 26.4 %rows.1 = (bf16[128,256,256]{2,1,0:T(8,128)(2,1)}, f32[128,256]{1,0:T(8,128)}, f32[128,256]{1,0:T(8,128)}) custom-call(s32[128]{0:T(128)} %reshape.43.listed, s32[16]{0:T(128)} %bitcast.14, f32[3,16,256]{2,1,0:T(8,128)} %sp.3, f32[3,256,256]{2,1,0:T(8,128)} %tp.3, f32[256,256]{1,0:T(8,128)} %tm.3, s32[128,1]{1,0:T(8,128)} %reshape.47.alive), custom_call_target="tpu_custom_call" | custom-call | flops 100000000 | bytes 10000000 | tf_op jit(solution)/shard_map/rows/pallas_call | solution.py:204
  44.9 0.0 all-to-all-done
  44.9 0.0 copy-start
  44.9 0.6 copy-done
  45.5 4.3 %coarse.1 = (f32[8,256]{1,0:T(8,128)}, f32[128,256]{1,0:T(8,128)}, f32[16,256]{1,0:T(8,128)}) custom-call(f32[128,128]{1,0:T(8,128)} %bitcast.11, f32[8,256]{1,0:T(8,128)} %get-tuple-element.13.own, f32[128,256]{1,0:T(8,128)} %get-tuple-element.14.m_in, f32[128,256]{1,0:T(8,128)} %get-tuple-element.15.r_in, s32[128,1]{1,0:T(8,128)} %reshape.48.listed), custom_call_target="tpu_custom_call" | custom-call | tf_op jit(solution)/shard_map/coarse/pallas_call | solution.py:220
  49.8 0.0 copy-start.4
  49.8 4.9 %collective-permute-start.2 = (f32[16,256]{1,0:T(8,128)}, f32[16,256]{1,0:T(8,128)S(1)}, u32[]{:S(2)}, u32[]{:S(2)}) collective-permute-start(f32[16,256]{1,0:T(8,128)} %get-tuple-element.17.l0), channel_id=1, source_target_pairs={{0,3},{1,0},{2,1},{3,2},{4,7},{5,4},{6,5},{7,6},{8,11},{9,8},{10,9... | collective-permute-start | bytes 49160 | tf_op jit(solution)/shard_map/ppermute | solution.py:228
  54.7 3.8 %collective-permute-start.1 = (f32[16,256]{1,0:T(8,128)}, f32[16,256]{1,0:T(8,128)S(1)}, u32[]{:S(2)}, u32[]{:S(2)}) collective-permute-start(f32[16,256]{1,0:T(8,128)} %get-tuple-element.17.l0), channel_id=1, source_target_pairs={{0,2},{1,3},{2,0},{3,1},{4,6},{5,7},{6,4},{7,5},{8,10},{9,11},{10,... | collective-permute-start | bytes 49160 | tf_op jit(solution)/shard_map/ppermute | solution.py:228
  58.6 0.8 collective-permute-start
  59.4 0.0 collective-permute-done.2.l3
  59.4 0.0 copy-start.1
  59.4 0.5 collective-permute-done.1.l2
  59.9 0.0 copy-start.2
  59.9 2.7 %collective-permute-done.l1 = f32[16,256]{1,0:T(8,128)S(1)} collective-permute-done((f32[16,256]{1,0:T(8,128)}, f32[16,256]{1,0:T(8,128)S(1)}, u32[]{:S(2)}, u32[]{:S(2)}) %collective-permute-start) | collective-permute-done | bytes 16416 | tf_op jit(solution)/shard_map/ppermute | solution.py:228
  62.6 0.0 copy-start.3
  62.6 0.0 copy-done.1
  62.6 0.0 copy-done.2
  62.6 0.6 copy-done.3
  63.2 16.5 %columns.1 = (f32[16,256]{1,0:T(8,128)}, f32[32,8,256]{2,1,0:T(8,128)}) custom-call(s32[128]{0:T(128)} %reshape.43.listed, s32[16]{0:T(128)} %bitcast.15, f32[16,256]{1,0:T(8,128)} %sm.3, f32[128,256]{1,0:T(8,128)} %get-tuple-element.16.mg, f32[16,256]{1,0:T(8,128)} %get-tuple-element.17.l0, f32[16,256]{1,0:T(8,128)} %copy-done.3, f32[16,256]{1,0:T(8,128)} %copy-done.2, ...), custom_call_target="tpu_custom_call" | custom-call | tf_op jit(solution)/shard_map/columns/pallas_call | solution.py:230
  79.7 17.6 %all-to-all-start.1 = ((f32[32,8,256]{2,1,0:T(8,128)}), f32[32,8,256]{2,1,0:T(8,128)S(1)}, u32[]{:S(2)}, u32[]{:S(2)}) async-start(f32[32,8,256]{2,1,0:T(8,128)} %get-tuple-element.21), calls=%async_computation.1 | async-start | bytes 524288 | tf_op jit(solution)/shard_map/all_to_all | solution.py:243
  97.3 9.0 %all-to-all-done.1 = f32[32,8,256]{2,1,0:T(8,128)S(1)} async-done(((f32[32,8,256]{2,1,0:T(8,128)}), f32[32,8,256]{2,1,0:T(8,128)S(1)}, u32[]{:S(2)}, u32[]{:S(2)}) %all-to-all-start.1) | async-done | bytes 262176 | tf_op jit(solution)/shard_map/all_to_all | solution.py:243
  106.3 0.0 copy-done.4
  106.3 1.3 %subtract_multiply_fusion = f32[8,256]{1,0:T(8,128)} fusion(f32[8,256]{1,0:T(8,128)S(1)} %copy-done.4, f32[8,256]{1,0:T(8,128)S(1)} %reduce_sum.9, f32[256,256]{1,0:T(8,128)} %tm.3, s32[]{:T(128)S(6)} %select_n.3), kind=kLoop, calls=%fused_computation | loop fusion | flops 10240 | bytes 32772 | tf_op jit(solution)/shard_map/mul | solution.py:245
  (1 shorter events, 0.0 us)
Async XLA Ops:
  3.4 41.5 %all-to-all-start = ((f32[128,1,128]{2,1,0:T(1,128)}), f32[128,1,128]{2,1,0:T(1,128)S(1)}, u32[]{:S(2)}, u32[]{:S(2)}) async-start(f32[128,1,128]{2,1,0:T(1,128)} %bitcast.12), calls=%async_computation | async-start | bytes 131072 | tf_op jit(solution)/shard_map/all_to_all | solution.py:199
  44.9 0.6 copy-start
  49.8 56.5 %copy-start.4 = (f32[8,256]{1,0:T(8,128)S(1)}, f32[8,256]{1,0:T(8,128)}, u32[]{:S(2)}) copy-start(f32[8,256]{1,0:T(8,128)} %get-tuple-element.20) | copy-start | bytes 24580
  49.8 9.6 %collective-permute-start.2 = (f32[16,256]{1,0:T(8,128)}, f32[16,256]{1,0:T(8,128)S(1)}, u32[]{:S(2)}, u32[]{:S(2)}) collective-permute-start(f32[16,256]{1,0:T(8,128)} %get-tuple-element.17.l0), channel_id=1, source_target_pairs={{0,3},{1,0},{2,1},{3,2},{4,7},{5,4},{6,5},{7,6},{8,11},{9,8},{10,9... | collective-permute-start | bytes 49160 | tf_op jit(solution)/shard_map/ppermute | solution.py:228
  54.7 5.2 %collective-permute-start.1 = (f32[16,256]{1,0:T(8,128)}, f32[16,256]{1,0:T(8,128)S(1)}, u32[]{:S(2)}, u32[]{:S(2)}) collective-permute-start(f32[16,256]{1,0:T(8,128)} %get-tuple-element.17.l0), channel_id=1, source_target_pairs={{0,2},{1,3},{2,0},{3,1},{4,6},{5,7},{6,4},{7,5},{8,10},{9,11},{10,... | collective-permute-start | bytes 49160 | tf_op jit(solution)/shard_map/ppermute | solution.py:228
  58.6 4.0 %collective-permute-start = (f32[16,256]{1,0:T(8,128)}, f32[16,256]{1,0:T(8,128)S(1)}, u32[]{:S(2)}, u32[]{:S(2)}) collective-permute-start(f32[16,256]{1,0:T(8,128)} %get-tuple-element.17.l0), channel_id=1, source_target_pairs={{0,1},{1,2},{2,3},{3,0},{4,5},{5,6},{6,7},{7,4},{8,9},{9,10},{10,1... | collective-permute-start | bytes 49160 | tf_op jit(solution)/shard_map/ppermute | solution.py:228
  59.4 3.2 %copy-start.1 = (f32[16,256]{1,0:T(8,128)}, f32[16,256]{1,0:T(8,128)S(1)}, u32[]{:S(2)}) copy-start(f32[16,256]{1,0:T(8,128)S(1)} %collective-permute-done.2.l3) | copy-start | bytes 49156
  59.9 2.7 %copy-start.2 = (f32[16,256]{1,0:T(8,128)}, f32[16,256]{1,0:T(8,128)S(1)}, u32[]{:S(2)}) copy-start(f32[16,256]{1,0:T(8,128)S(1)} %collective-permute-done.1.l2) | copy-start | bytes 49156
  62.6 0.6 copy-start.3
  79.7 26.6 %all-to-all-start.1 = ((f32[32,8,256]{2,1,0:T(8,128)}), f32[32,8,256]{2,1,0:T(8,128)S(1)}, u32[]{:S(2)}, u32[]{:S(2)}) async-start(f32[32,8,256]{2,1,0:T(8,128)} %get-tuple-element.21), calls=%async_computation.1 | async-start | bytes 524288 | tf_op jit(solution)/shard_map/all_to_all | solution.py:243

commit v2 on v1

v2 whole, which is shorter than its diff:
```python
import functools
import math

import jax
import jax.numpy as jnp
from jax import lax
from jax.experimental import pallas as pl
from jax.experimental.pallas import tpu as pltpu
from jax.sharding import PartitionSpec as P

EPS = 0.1
NEG = -1e30
ALPHA = math.log2(math.e) / EPS
UNSCALE = EPS * math.log(2.0)
F32, BF16, I32 = jnp.float32, jnp.bfloat16, jnp.int32
CL, SLOTS, PTS, TGT = 16, 8, 256, 256
BLOCKS = CL * SLOTS
UNROLL = 4
PAD = 8
VMEM_LIMIT = 24 << 20
VMEM = pl.BlockSpec(memory_space=pltpu.VMEM)
SMEM = pl.BlockSpec(memory_space=pltpu.SMEM)
ANY = pl.BlockSpec(memory_space=pl.ANY)


def iota(shape, dim):
    return lax.broadcasted_iota(I32, shape, dim)


def split3(value):
    high = value.astype(BF16).astype(F32)
    rest = value - high
    mid = rest.astype(BF16).astype(F32)
    return high, mid, rest - mid


def centroid_kernel(sp, sm, tp, tm, row_out, own_out):
    s, t = lax.axis_index("src"), lax.axis_index("tgt")
    mass = sm[...]
    total = jnp.sum(mass, axis=1, keepdims=True)
    inv = 1.0 / total
    cols = [jnp.sum(sp[d] * mass, axis=1, keepdims=True) * inv for d in range(3)]
    cols.append(jnp.log2(total))
    lane = iota((CL, 128), 1)
    z = jnp.zeros((CL, 128), F32)
    for q in range(4):
        z = jnp.where(lane == q, cols[q], z)
    zt = jnp.concatenate([z, jnp.zeros((128 - CL, 128), F32)], axis=0).T
    lane = iota((1, 128), 1)
    row = jnp.zeros((1, 128), F32)
    for q in range(4):
        piece = pltpu.roll(zt[q : q + 1, :], lax.rem(128 - 4 * t, 128), 1)
        row = row + pltpu.roll(jnp.where(lane < 4, piece, 0.0), 4 * q, 1)
    weight = tm[...]
    total = jnp.sum(weight, axis=0, keepdims=True)
    inv = 1.0 / total
    rows = [jnp.sum(tp[d] * weight, axis=0, keepdims=True) * inv for d in range(3)]
    rows.append(jnp.log2(total))
    for q in range(4):
        own_out[q : q + 1, :] = rows[q]
        half = jnp.where(s >= 16, rows[q][:, 128:], rows[q][:, :128])
        piece = pltpu.roll(half, lax.rem(128 - 8 * lax.rem(s, 16), 128), 1)
        row = row + pltpu.roll(jnp.where(lane < 8, piece, 0.0), 16 + 8 * q, 1)
    row_out[...] = jnp.broadcast_to(row, row_out.shape)


def row_kernel(listed, live, sp, tp, tm, e_out, m_out, r_out, l_out, order, gt, gf, tab, lhs_a, lhs_b, score_a, score_b, tops_a, tops_b, scol, lrow):
    n = 0
    for c in range(CL):
        for k in range(SLOTS):
            order[n + k] = k * CL + c
        n = n + live[0, c]
    for u in range(PAD):
        order[n + u] = order[0]
    order[BLOCKS + PAD] = n

    for d in range(3):
        a, b, _ = split3(sp[d] * ALPHA)
        for r, piece in enumerate((a, b, a, b)):
            for h in range(2):
                gf[h, pl.ds(4 * d + r, CL, stride=16), :] = piece[:, 128 * h : 128 * h + 128]
    for r in range(12, 16):
        for h in range(2):
            gf[h, pl.ds(r, CL, stride=16), :] = jnp.full((CL, 128), 1.0 if r < 15 else 0.0, F32)
    for c in range(CL):
        gt[c] = jnp.concatenate([gf[h, 16 * c : 16 * c + 16, :] for h in range(2)], axis=1).astype(BF16)
    for d in range(3):
        a, b, _ = split3(tp[d].T)
        tab[2 * d] = a
        tab[2 * d + 1] = b
    base = -(0.5 * ALPHA) * (tp[0] * tp[0] + tp[1] * tp[1] + tp[2] * tp[2]) + jnp.log2(tm[...])
    for r, piece in enumerate(split3(base.T)):
        tab[6 + r] = piece
    sub = iota((16, PTS), 0)
    source = [0, 0, 1, 1, 2, 2, 3, 3, 4, 4, 5, 5, 6, 7, 8]

    def prepare(i, lhs):
        b = order[i]
        at = listed[b // CL, lax.rem(b, CL)]
        pieces = [tab[q, pl.ds(at, 1), :] for q in range(9)]
        stack = jnp.zeros((16, PTS), F32)
        for r, q in enumerate(source):
            stack = jnp.where(sub == r, pieces[q], stack)
        lhs[...] = stack.T.astype(BF16)
        lrow[pl.ds(b, 1), :] = jnp.broadcast_to(at.astype(F32), (1, 128))

    sets = ((lhs_a, score_a, tops_a), (lhs_b, score_b, tops_b))
    for u in range(2):
        prepare(u, sets[u][0])

    def pair(i, _):
        old = [order[jnp.maximum(2 * i - 2 + u, 0)] for u in range(2)]
        v = [jnp.dot(sets[u][0][...], gt[lax.rem(order[2 * i + u], CL)], preferred_element_type=F32) for u in range(2)]
        top_old = [sets[u][2][...] for u in range(2)]
        total = [jnp.zeros((8, PTS), F32) for u in range(2)]
        top = [jnp.full((8, PTS), NEG, F32) for u in range(2)]
        for u in range(2):
            prepare(2 * i + 2 + u, sets[u][0])
        for j in range(0, TGT, 32):
            for u in range(2):
                score = sets[u][1]
                es = []
                for o in range(j, j + 32, 8):
                    e = jnp.exp2(score[o : o + 8, :] - top_old[u])
                    total[u] = total[u] + e
                    es.append(e)
                e_out[old[u], j : j + 32, :] = jnp.concatenate(es, axis=0).astype(BF16)
                score[j : j + 32, :] = v[u][j : j + 32, :]
                for o in range(j, j + 32, 8):
                    top[u] = jnp.maximum(top[u], v[u][o : o + 8, :])
        for u in range(2):
            sets[u][2][...] = jnp.broadcast_to(jnp.max(top[u], axis=0, keepdims=True), (8, PTS))
            scol[pl.ds(old[u], 1), :] = jnp.sum(total[u], axis=0, keepdims=True)
            m_out[pl.ds(old[u], 1), :] = top_old[u][0:1, :]
        return 0

    lax.fori_loop(0, (n + 1) // 2 + 1, pair, 0)
    xn = (-0.5 * ALPHA) * (sp[0] * sp[0] + sp[1] * sp[1] + sp[2] * sp[2])
    lane = iota((1, 128), 1)
    have = jnp.zeros((1, 128), I32)
    for c in range(CL):
        have = jnp.where((lane & (CL - 1)) == c, live[0, c], have)
    ok = jnp.broadcast_to(jnp.where((lane >> 4) < have, 1.0, 0.0), (128, 128)).T[:, 0:1] > 0.5
    m = (m_out[...].reshape(SLOTS, CL, PTS) + xn[None]).reshape(BLOCKS, PTS)
    m_out[...] = m
    r_out[...] = jnp.where(ok, m + jnp.log2(scol[...]), NEG)
    l_out[...] = jnp.where(ok, lrow[...], -1.0)


def coarse_kernel(got, own, m_in, r_in, l_in, g_out, mg_out, l_out, terms):
    turned = got[...].T

    def side(rows):
        norm = rows[0] * rows[0] + rows[1] * rows[1] + rows[2] * rows[2]
        return [rows[0], rows[1], rows[2], rows[3] - (0.5 * ALPHA) * norm]

    tgt = [side([turned[16 + 8 * q + li : 17 + 8 * q + li, :] for q in range(4)]) for li in range(8)]
    mine = side([own[q : q + 1, :] for q in range(4)])
    top_g = jnp.full((16, TGT), NEG, F32)
    for ci in range(4):
        for i in range(0, 128, 16):
            x = [jnp.broadcast_to(got[i : i + 16, 4 * d + ci : 4 * d + ci + 1], (16, 128)) for d in range(3)]
            mass = got[i : i + 16, 12 + ci : 13 + ci]
            ax = [ALPHA * v for v in x]
            scores = [y[3] + ax[0] * y[0] + ax[1] * y[1] + ax[2] * y[2] for y in tgt]
            top = jnp.max(functools.reduce(jnp.maximum, scores), axis=1, keepdims=True)
            total = jnp.sum(sum(jnp.exp2(v - top) for v in scores), axis=1, keepdims=True)
            const = mass - (top + jnp.log2(total))
            halves = []
            for h in (0, 128):
                y = [row[:, h : h + 128] for row in mine]
                halves.append(const + ax[0] * y[0] + ax[1] * y[1] + ax[2] * y[2])
            v = jnp.concatenate(halves, axis=1)
            terms[128 * ci + i : 128 * ci + i + 16, :] = v
            top_g = jnp.maximum(top_g, v)
    top = jnp.max(top_g, axis=0, keepdims=True)
    total = jnp.zeros((16, TGT), F32)
    for i in range(0, 512, 16):
        total = total + jnp.exp2(terms[i : i + 16, :] - top)
    g = (mine[3] - own[3:4, :]) + top + jnp.log2(jnp.sum(total, axis=0, keepdims=True))
    g = -g
    g_out[...] = jnp.broadcast_to(g, g_out.shape)
    at = l_in[...]
    lane = iota((128, 128), 1).astype(F32)
    hit = jnp.where(at == lane, g[:, :128], 0.0) + jnp.where(at == lane + 128.0, g[:, 128:], 0.0)
    picked = jnp.sum(hit, axis=1, keepdims=True)
    mg_out[...] = m_in[...] + picked
    r = (r_in[...] + picked).reshape(SLOTS, CL, PTS)
    top = jnp.max(r, axis=0)
    l_out[...] = top + jnp.log2(jnp.sum(jnp.exp2(r - top[None]), axis=0))


def column_kernel(order, sm, mg, l0, l1, l2, l3, at, e_in, f_out, s_out, sums):
    n = order[BLOCKS + PAD]
    parts = [p[...] for p in (l0, l1, l2, l3)]
    top = functools.reduce(jnp.maximum, parts)
    f = -(top + jnp.log2(sum(jnp.exp2(p - top) for p in parts)))
    f_out[...] = f * UNSCALE
    weights = sm[...][None] * jnp.exp2(mg[...].reshape(SLOTS, CL, PTS) + f[None])
    alive = at[...][:, 0:1] >= 0.0
    w = jnp.where(alive, weights.reshape(BLOCKS, PTS), 0.0).T
    high = w.astype(BF16)
    w = jnp.concatenate([high, (w - high.astype(F32)).astype(BF16)], axis=1)
    sums[...] = jnp.zeros_like(sums)
    lane = iota((TGT, 128), 1)

    def group(g, _):
        for u in range(UNROLL):
            b = order[g * UNROLL + u]
            out = jnp.dot(e_in[b], w, preferred_element_type=F32)
            pltpu.store(sums, out[:, :128] + out[:, 128:], mask=lane == b)
        return 0

    lax.fori_loop(0, (n + UNROLL - 1) // UNROLL, group, 0)
    lane = iota((128, TGT), 1).astype(F32)
    own = jnp.where(lane == jnp.concatenate([at[...], at[...]], axis=1), 1.0, 0.0).astype(BF16)
    total = jnp.zeros((TGT, TGT), F32)
    for piece in split3(sums[...]):
        total = total + jnp.dot(piece.astype(BF16), own, preferred_element_type=F32)
    s_out[...] = total.reshape(32, 8, TGT)


def on_device(src_pts, src_mass, tgt_pts, tgt_mass, listed, live):
    shape = jax.ShapeDtypeStruct
    row, own = pl.pallas_call(
        centroid_kernel,
        out_shape=(shape((128, 128), F32), shape((8, 256), F32)),
        in_specs=[VMEM] * 4,
        out_specs=(VMEM, VMEM),
        name="centroids",
    )(src_pts, src_mass, tgt_pts, tgt_mass)
    got = lax.all_to_all(row, ("src", "tgt"), split_axis=0, concat_axis=0, tiled=True)
    slots = listed.transpose(1, 2, 0).reshape(SLOTS, CL)
    counts = live.transpose(1, 0)
    e, m, r, where, order = pl.pallas_call(
        row_kernel,
        out_shape=(
            pltpu.VMEM((BLOCKS, TGT, PTS), BF16),
            shape((BLOCKS, PTS), F32),
            shape((BLOCKS, PTS), F32),
            shape((128, 128), F32),
            shape((BLOCKS + 2 * PAD,), I32),
        ),
        in_specs=[SMEM, SMEM, VMEM, VMEM, VMEM],
        out_specs=(VMEM, VMEM, VMEM, VMEM, SMEM),
        scratch_shapes=[
            pltpu.VMEM((CL, 16, PTS), BF16),
            pltpu.VMEM((2, CL * 16, 128), F32),
            pltpu.VMEM((9, TGT, PTS), F32),
            pltpu.VMEM((TGT, 16), BF16),
            pltpu.VMEM((TGT, 16), BF16),
            pltpu.VMEM((TGT, PTS), F32),
            pltpu.VMEM((TGT, PTS), F32),
            pltpu.VMEM((8, PTS), F32),
            pltpu.VMEM((8, PTS), F32),
            pltpu.VMEM((BLOCKS, PTS), F32),
            pltpu.VMEM((BLOCKS, 128), F32),
        ],
        cost_estimate=pl.CostEstimate(flops=100_000_000, bytes_accessed=10_000_000, transcendentals=5_000_000),
        compiler_params=pltpu.CompilerParams(vmem_limit_bytes=VMEM_LIMIT),
        name="rows",
    )(slots, counts, src_pts, tgt_pts, tgt_mass)
    g, mg, part = pl.pallas_call(
        coarse_kernel,
        out_shape=(shape((8, 256), F32), shape((BLOCKS, PTS), F32), shape((CL, PTS), F32)),
        in_specs=[VMEM] * 5,
        out_specs=(VMEM, VMEM, VMEM),
        scratch_shapes=[pltpu.VMEM((512, 256), F32)],
        compiler_params=pltpu.CompilerParams(vmem_limit_bytes=VMEM_LIMIT),
        name="coarse",
    )(got, own, m, r, where)
    parts = [part] + [
        lax.ppermute(part, "tgt", [(i, (i + k) % 4) for i in range(4)]) for k in (1, 2, 3)
    ]
    fine_f, sums = pl.pallas_call(
        column_kernel,
        out_shape=(shape((CL, PTS), F32), shape((32, 8, TGT), F32)),
        in_specs=[SMEM] + [VMEM] * 8,
        out_specs=(VMEM, VMEM),
        scratch_shapes=[pltpu.VMEM((TGT, 128), F32)],
        compiler_params=pltpu.CompilerParams(vmem_limit_bytes=VMEM_LIMIT),
        name="columns",
    )(order, src_mass, mg, *parts, where, e)
    arrived = lax.all_to_all(sums, "src", split_axis=0, concat_axis=0, tiled=True)
    mass = lax.dynamic_slice_in_dim(tgt_mass, lax.axis_index("src") * 8, 8, 0)
    fine_g = (g - jnp.log2(1.0 + arrived.sum(axis=0) / mass)) * UNSCALE
    return fine_f, fine_g


def solution(mesh):
    placed = (
        P(None, "src", None),
        P("src", None),
        P(None, None, "tgt"),
        P(None, "tgt"),
        P("src", "tgt", None),
        P("src", "tgt"),
    )
    return jax.shard_map(
        on_device,
        mesh=mesh,
        in_specs=placed,
        out_specs=(P("src", None), P("src", "tgt")),
        check_vma=False,
    )
```

time: 108 us -> 79.9 us (0.74)
  Pallas kernels: 49.4 us -> 22.2 us
  starting transfers between devices: 38.7 us -> 25.3 us
  local copies, waits for them, and re-layouts: 4.04 us -> 17.1 us
  other arithmetic: 2.67 us -> 1.36 us
    pallas_call x3, Pallas kernels: 47.2 us -> 20 us  [the longest x1 8.6 us: on_device(): pl.pallas_call(row_kernel, out_shape=(pltpu.VMEM((BLOCKS, TGT, PTS), BF16...]
    unnamed x11 -> x18, local copies, waits for them, and re-layouts: 1.97 us -> 17.1 us
    all_to_all x1, starting transfers between devices: 17.6 us -> 7.6 us  [on_device(): lax.all_to_all(sums, 'src', split_axis=0, concat_axis=0, tiled=True)]
    ppermute x3, starting transfers between devices: 9.62 us -> 6.21 us  [on_device(): lax.ppermute(part, 'tgt', [(i, (i + k) % 4) for i in range(4)])]
    reshape x2 -> x0, local copies, waits for them, and re-layouts: 1.37 us -> none  [the longest x1 0.7 us: on_device(): column = listed.reshape(128, 1)]
  transfers between devices with their start and end apart: 5 -> 5, of which waited for: 3 -> 4; matrix products, arithmetic and copies ran while one was open for 3% -> 0% of each run, Pallas kernels for 25% -> 11%
where the time goes in v2:
time: 79.9 us; the launch traced here: 78.6 us
  starting transfers between devices  25.3 us (32%)
  Pallas kernels  22.2 us (28%)
  local copies, waits for them, and re-layouts  17.1 us (21%)
  waiting for transfers between devices  11.9 us (15%)
  other arithmetic  1.36 us (2%)
    unnamed x18, local copies, waits for them, and re-layouts  17.1 us
    all_to_all x1, starting transfers between devices, on_device(): lax.all_to_all(row, ('src', 'tgt'), split_axis=0, concat_axis=0, tiled=True)  11.5 us
    all_to_all x1, waiting for transfers between devices, on_device(): lax.all_to_all(sums, 'src', split_axis=0, concat_axis=0, tiled=True)  8.96 us
    pallas_call x1, Pallas kernels, on_device(): pl.pallas_call(row_kernel, out_shape=(pltpu.VMEM((BLOCKS, TGT, PTS), BF16...  8.6 us
    all_to_all x1, starting transfers between devices, on_device(): lax.all_to_all(sums, 'src', split_axis=0, concat_axis=0, tiled=True)  7.6 us
    pallas_call x1, Pallas kernels, on_device(): pl.pallas_call(column_kernel, out_shape=(shape((CL, PTS), F32), shape((32...  6.5 us
    ppermute x3, starting transfers between devices, on_device(): lax.ppermute(part, 'tgt', [(i, (i + k) % 4) for i in range(4)])  6.21 us
    pallas_call x1, Pallas kernels, on_device(): pl.pallas_call(coarse_kernel, out_shape=(shape((8, 256), F32), shape((BLO...  4.95 us
  transfers between devices with their start and end apart: 5, of which 4 were waited for; matrix products, arithmetic and copies ran while one was open for 0% of the time, Pallas kernels for 11%

profile of v2, /device:TPU:1, one launch (start us, length us, event | category | flops | bytes accessed | tf_op | source)
XLA Modules:
  0.0 78.6 jit_solution(14753229522075484311)
XLA Ops:
  0.6 2.2 %centroids.1 = (f32[128,128]{1,0:T(8,128)}, f32[8,256]{1,0:T(8,128)}) custom-call(f32[3,16,256]{2,1,0:T(8,128)} %sp.3, f32[16,256]{1,0:T(8,128)} %sm.3, f32[3,256,256]{2,1,0:T(8,128)} %tp.3, f32[256,256]{1,0:T(8,128)} %tm.3), custom_call_target="tpu_custom_call" | custom-call | tf_op jit(solution)/shard_map/centroids/pallas_call | solution.py:225
  2.8 11.5 %all-to-all-start = ((f32[128,1,128]{2,1,0:T(1,128)}), f32[128,1,128]{2,1,0:T(1,128)S(1)}, u32[]{:S(2)}, u32[]{:S(2)}) async-start(f32[128,1,128]{2,1,0:T(1,128)} %bitcast.11), calls=%async_computation | async-start | bytes 131072 | tf_op jit(solution)/shard_map/all_to_all | solution.py:232
  14.3 0.0 copy-start.2
  14.3 1.1 %copy-done.2 = f32[3,256,256]{2,1,0:T(8,128)S(1)} copy-done((f32[3,256,256]{2,1,0:T(8,128)S(1)}, f32[3,256,256]{2,1,0:T(8,128)}, u32[]{:S(2)}) %copy-start.2) | copy-done | bytes 786456
  15.4 0.0 copy-start.3
  15.4 0.9 %copy-done.3 = f32[256,256]{1,0:T(8,128)S(1)} copy-done((f32[256,256]{1,0:T(8,128)S(1)}, f32[256,256]{1,0:T(8,128)}, u32[]{:S(2)}) %copy-start.3) | copy-done | bytes 262168
  16.4 0.0 copy-start.5
  16.4 0.8 %copy-done.5 = f32[3,16,256]{2,1,0:T(8,128)S(1)} copy-done((f32[3,16,256]{2,1,0:T(8,128)S(1)}, f32[3,16,256]{2,1,0:T(8,128)}, u32[]{:S(2)}) %copy-start.5) | copy-done | bytes 49176
  17.2 0.0 copy-start.7
  17.2 0.7 copy-done.7
  17.9 0.0 copy-start.8
  17.9 0.7 copy-done.8
  18.5 8.6 %rows.1 = (bf16[128,256,256]{2,1,0:T(8,128)(2,1)S(1)}, f32[128,256]{1,0:T(8,128)S(1)}, f32[128,256]{1,0:T(8,128)S(1)}, f32[128,128]{1,0:T(8,128)S(1)}, s32[144]{0:T(256)S(1)}) custom-call(s32[8,16]{1,0:T(8,128)S(1)} %bitcast.9, s32[1,16]{1,0:T(1,128)S(1)} %bitcast.10, f32[3,16,256]{2,1,0:T(8,128)S(1)} %copy-done.5, f32[3,256,256]{2,1,0:T(8,128)S(1)} %copy-done.2, ...), custom_call_target="tpu_custom_call" | custom-call | flops 100000000 | bytes 10000000 | tf_op jit(solution)/shard_map/rows/pallas_call | solution.py:235
  27.1 0.0 copy-start
  27.1 5.7 %copy-done = bf16[128,256,256]{2,1,0:T(8,128)(2,1)} copy-done((bf16[128,256,256]{2,1,0:T(8,128)(2,1)}, bf16[128,256,256]{2,1,0:T(8,128)(2,1)S(1)}, u32[]{:S(2)}) %copy-start) | copy-done | bytes 16777240
  32.9 0.0 all-to-all-done
  32.9 0.0 copy-start.6
  32.9 0.7 copy-done.6
  33.6 4.9 %coarse.1 = (f32[8,256]{1,0:T(8,128)S(1)}, f32[128,256]{1,0:T(8,128)S(1)}, f32[16,256]{1,0:T(8,128)S(1)}) custom-call(f32[128,128]{1,0:T(8,128)S(1)} %bitcast.8, f32[8,256]{1,0:T(8,128)S(1)} %copy-done.6, f32[128,256]{1,0:T(8,128)S(1)} %get-tuple-element.17.m_in, f32[128,256]{1,0:T(8,128)S(1)} %get-tuple-element.18.r_in, ...), custom_call_target="tpu_custom_call" | custom-call | tf_op jit(solution)/shard_map/coarse/pallas_call | solution.py:263
  38.5 1.6 %collective-permute-start = (f32[16,256]{1,0:T(8,128)S(1)}, f32[16,256]{1,0:T(8,128)S(1)}, u32[]{:S(2)}, u32[]{:S(2)}) collective-permute-start(f32[16,256]{1,0:T(8,128)S(1)} %get-tuple-element.21.l0), channel_id=1, source_target_pairs={{0,1},{1,2},{2,3},{3,0},{4,5},{5,6},{6,7},{7,4},{8,9},{9,10},{10,1... | collective-permute-start | bytes 49160 | tf_op jit(solution)/shard_map/ppermute | solution.py:273
  40.2 4.6 %collective-permute-start.1 = (f32[16,256]{1,0:T(8,128)S(1)}, f32[16,256]{1,0:T(8,128)S(1)}, u32[]{:S(2)}, u32[]{:S(2)}) collective-permute-start(f32[16,256]{1,0:T(8,128)S(1)} %get-tuple-element.21.l0), channel_id=1, source_target_pairs={{0,2},{1,3},{2,0},{3,1},{4,6},{5,7},{6,4},{7,5},{8,10},{9,11},{10,... | collective-permute-start | bytes 49160 | tf_op jit(solution)/shard_map/ppermute | solution.py:273
  44.8 0.0 collective-permute-start.2
  44.8 0.2 collective-permute-done.l1
  44.9 1.1 %collective-permute-done.1.l2 = f32[16,256]{1,0:T(8,128)S(1)} collective-permute-done((f32[16,256]{1,0:T(8,128)S(1)}, f32[16,256]{1,0:T(8,128)S(1)}, u32[]{:S(2)}, u32[]{:S(2)}) %collective-permute-start.1) | collective-permute-done | bytes 16416 | tf_op jit(solution)/shard_map/ppermute | solution.py:273
  46.1 1.6 %collective-permute-done.2.l3 = f32[16,256]{1,0:T(8,128)S(1)} collective-permute-done((f32[16,256]{1,0:T(8,128)S(1)}, f32[16,256]{1,0:T(8,128)S(1)}, u32[]{:S(2)}, u32[]{:S(2)}) %collective-permute-start.2) | collective-permute-done | bytes 16416 | tf_op jit(solution)/shard_map/ppermute | solution.py:273
  47.7 0.0 copy-start.1
  47.7 5.8 %copy-done.1 = bf16[128,256,256]{2,1,0:T(8,128)(2,1)S(1)} copy-done((bf16[128,256,256]{2,1,0:T(8,128)(2,1)S(1)}, bf16[128,256,256]{2,1,0:T(8,128)(2,1)}, u32[]{:S(2)}) %copy-start.1) | copy-done | bytes 16777240
  53.5 0.0 copy-start.4
  53.5 0.7 copy-done.4
  54.2 6.5 %columns.1 = (f32[16,256]{1,0:T(8,128)}, f32[32,8,256]{2,1,0:T(8,128)}) custom-call(s32[144]{0:T(256)S(1)} %get-tuple-element.14.order, f32[16,256]{1,0:T(8,128)S(1)} %copy-done.4, f32[128,256]{1,0:T(8,128)S(1)} %get-tuple-element.20.mg, f32[16,256]{1,0:T(8,128)S(1)} %get-tuple-element.21.l0, f32[16,256]{1,0:T(8,128)S(1)} %collective-permute-done.l1, ...), custom_call_target="tpu_custom_call" | custom-call | tf_op jit(solution)/shard_map/columns/pallas_call | solution.py:275
  60.7 7.6 %all-to-all-start.1 = ((f32[32,8,256]{2,1,0:T(8,128)}), f32[32,8,256]{2,1,0:T(8,128)S(1)}, u32[]{:S(2)}, u32[]{:S(2)}) async-start(f32[32,8,256]{2,1,0:T(8,128)} %get-tuple-element.25), calls=%async_computation.1 | async-start | bytes 524288 | tf_op jit(solution)/shard_map/all_to_all | solution.py:284
  68.3 9.0 %all-to-all-done.1 = f32[32,8,256]{2,1,0:T(8,128)S(1)} async-done(((f32[32,8,256]{2,1,0:T(8,128)}), f32[32,8,256]{2,1,0:T(8,128)S(1)}, u32[]{:S(2)}, u32[]{:S(2)}) %all-to-all-start.1) | async-done | bytes 262176 | tf_op jit(solution)/shard_map/all_to_all | solution.py:284
  77.3 1.3 %subtract_multiply_fusion = f32[8,256]{1,0:T(8,128)} fusion(f32[8,256]{1,0:T(8,128)S(1)} %get-tuple-element.24, f32[8,256]{1,0:T(8,128)S(1)} %reduce_sum.9, f32[256,256]{1,0:T(8,128)} %tm.3, s32[]{:T(128)S(6)} %select_n.3), kind=kLoop, calls=%fused_computation | loop fusion | flops 10240 | bytes 32772 | tf_op jit(solution)/shard_map/mul | solution.py:286
  (1 shorter events, 0.0 us)
Async XLA Ops:
  2.8 30.1 %all-to-all-start = ((f32[128,1,128]{2,1,0:T(1,128)}), f32[128,1,128]{2,1,0:T(1,128)S(1)}, u32[]{:S(2)}, u32[]{:S(2)}) async-start(f32[128,1,128]{2,1,0:T(1,128)} %bitcast.11), calls=%async_computation | async-start | bytes 131072 | tf_op jit(solution)/shard_map/all_to_all | solution.py:232
  14.3 1.1 %copy-start.2 = (f32[3,256,256]{2,1,0:T(8,128)S(1)}, f32[3,256,256]{2,1,0:T(8,128)}, u32[]{:S(2)}) copy-start(f32[3,256,256]{2,1,0:T(8,128)} %tp.3) | copy-start | bytes 2359300
  15.4 0.9 %copy-start.3 = (f32[256,256]{1,0:T(8,128)S(1)}, f32[256,256]{1,0:T(8,128)}, u32[]{:S(2)}) copy-start(f32[256,256]{1,0:T(8,128)} %tm.3) | copy-start | bytes 786436
  16.4 0.8 %copy-start.5 = (f32[3,16,256]{2,1,0:T(8,128)S(1)}, f32[3,16,256]{2,1,0:T(8,128)}, u32[]{:S(2)}) copy-start(f32[3,16,256]{2,1,0:T(8,128)} %sp.3) | copy-start | bytes 147460
  17.2 0.7 copy-start.7
  17.9 0.7 copy-start.8
  27.1 5.7 %copy-start = (bf16[128,256,256]{2,1,0:T(8,128)(2,1)}, bf16[128,256,256]{2,1,0:T(8,128)(2,1)S(1)}, u32[]{:S(2)}) copy-start(bf16[128,256,256]{2,1,0:T(8,128)(2,1)S(1)} %get-tuple-element.22.e_in) | copy-start | bytes 50331652
  32.9 0.7 copy-start.6
  38.5 6.4 %collective-permute-start = (f32[16,256]{1,0:T(8,128)S(1)}, f32[16,256]{1,0:T(8,128)S(1)}, u32[]{:S(2)}, u32[]{:S(2)}) collective-permute-start(f32[16,256]{1,0:T(8,128)S(1)} %get-tuple-element.21.l0), channel_id=1, source_target_pairs={{0,1},{1,2},{2,3},{3,0},{4,5},{5,6},{6,7},{7,4},{8,9},{9,10},{10,1... | collective-permute-start | bytes 49160 | tf_op jit(solution)/shard_map/ppermute | solution.py:273
  40.2 5.9 %collective-permute-start.1 = (f32[16,256]{1,0:T(8,128)S(1)}, f32[16,256]{1,0:T(8,128)S(1)}, u32[]{:S(2)}, u32[]{:S(2)}) collective-permute-start(f32[16,256]{1,0:T(8,128)S(1)} %get-tuple-element.21.l0), channel_id=1, source_target_pairs={{0,2},{1,3},{2,0},{3,1},{4,6},{5,7},{6,4},{7,5},{8,10},{9,11},{10,... | collective-permute-start | bytes 49160 | tf_op jit(solution)/shard_map/ppermute | solution.py:273
  44.8 2.9 %collective-permute-start.2 = (f32[16,256]{1,0:T(8,128)S(1)}, f32[16,256]{1,0:T(8,128)S(1)}, u32[]{:S(2)}, u32[]{:S(2)}) collective-permute-start(f32[16,256]{1,0:T(8,128)S(1)} %get-tuple-element.21.l0), channel_id=1, source_target_pairs={{0,3},{1,0},{2,1},{3,2},{4,7},{5,4},{6,5},{7,6},{8,11},{9,8},{10,9... | collective-permute-start | bytes 49160 | tf_op jit(solution)/shard_map/ppermute | solution.py:273
  47.7 5.8 %copy-start.1 = (bf16[128,256,256]{2,1,0:T(8,128)(2,1)S(1)}, bf16[128,256,256]{2,1,0:T(8,128)(2,1)}, u32[]{:S(2)}) copy-start(bf16[128,256,256]{2,1,0:T(8,128)(2,1)} %copy-done) | copy-start | bytes 50331652
  53.5 0.7 copy-start.4
  60.7 16.6 %all-to-all-start.1 = ((f32[32,8,256]{2,1,0:T(8,128)}), f32[32,8,256]{2,1,0:T(8,128)S(1)}, u32[]{:S(2)}, u32[]{:S(2)}) async-start(f32[32,8,256]{2,1,0:T(8,128)} %get-tuple-element.25), calls=%async_computation.1 | async-start | bytes 524288 | tf_op jit(solution)/shard_map/all_to_all | solution.py:284
